TPU v7x, 256 devices: a whole 4x4x8 slice. The times are simulated.
256 devices in a mesh: seq: 16 (over x, y), exp: 16 (over z, core).
Axes of the slice: x: 4, y: 4, z: 8, core: 2. Of those that a mesh axis runs over, the one named last changes fastest.
Arguments:
- tokens: bfloat16 [32, 1024, 1152], P('exp', 'seq'), may hold values from -80 to 80
- timesteps: int32 [32], P('exp'), may hold values from 0 to 63
- modulation: bfloat16 [64, 2, 1152], replicated, may hold values from -0.5 to 0.5
- routes: int32 [16, 1024, 2, 2], P('exp', 'seq'), may hold values from 0 to 15, all different within a row; in each aligned block of 128 rows (0 to 127, 128 to 255, ..., all dimensions but the last counted through in order) at most 17 rows name the same one
- gate_codes: int32 [32, 1024, 2], P('exp', 'seq'), may hold values from 1 to 16
- gate_weight: bfloat16 [16, 1152, 4608], P('exp', None, 'seq'), may hold values from -0.1875 to 0.1875
- up_weight: bfloat16 [16, 1152, 4608], P('exp', None, 'seq'), may hold values from -0.1875 to 0.1875
- down_weight: bfloat16 [16, 4608, 1152], P('exp', 'seq'), may hold values from -0.09375 to 0.09375
- cotangent: bfloat16 [32, 1024, 1152], P('exp', 'seq'), may hold values from -6 to 6
Outputs:
- grad_tokens: bfloat16 [32, 1024, 1152], P('exp', 'seq')
Inputs may be any that keep to these rules, and one draw needn't show every extreme that they name: `routes`: among the rows of one device (entries [g, p, i, :] with p in one block of 64 patches, all i) no expert is named more than 17 times, a bound that some block reaches.
All inputs are finite; a program needn't handle non-finite values.
Results may differ from a plain program's by a relative error of at most 0.015.
Values may be sent and summed in bfloat16 or wider, within the bound.
A program may use at most 192 MiB of HBM per device.

v0:
```python
import jax
import jax.numpy as jnp
from jax import lax
from jax.sharding import PartitionSpec as P


def in_one_piece(arrays, axis, split_dim, concat_dim, along):
    ends, at = ([], 0)
    for a in arrays[:-1]:
        at += a.shape[along]
        ends.append(at)
    both = jnp.concatenate(arrays, axis=along)
    return tuple(
        jnp.split(
            lax.all_to_all(both, axis, split_axis=split_dim, concat_axis=concat_dim, tiled=True),
            ends,
            axis=along,
        )
    )


def normalize_modulate(tokens_f, shift, scale):
    mean_square = jnp.mean(tokens_f * tokens_f, axis=-1, keepdims=True)
    return tokens_f / jnp.sqrt(mean_square + 1e-06) * (1.0 + scale) + shift


def per_device(
    tokens,
    timesteps,
    modulation,
    routes,
    gate_codes,
    gate_weight,
    up_weight,
    down_weight,
    cotangent,
):
    img_local, patch_local, feature_width = tokens.shape
    top_count = routes.shape[3]
    row_count = img_local * patch_local
    n_exp = lax.axis_size("exp")
    local_experts = gate_weight.shape[0]
    block_width = gate_weight.shape[2]
    expert_count = local_experts * n_exp
    capacity = top_count * row_count // expert_count + 1
    slot_count = expert_count * capacity
    level_count = modulation.shape[0]
    select = (timesteps[:, None] == jnp.arange(level_count, dtype=jnp.int32)[None, :]).astype(
        jnp.float32
    )
    table = jnp.dot(
        select,
        modulation.astype(jnp.float32).reshape(level_count, 2 * feature_width),
        precision=lax.Precision.HIGHEST,
    )
    table = jnp.broadcast_to(
        table[:, None, :], (img_local, patch_local, 2 * feature_width)
    ).reshape(row_count, 2 * feature_width)
    scale = table[:, :feature_width]
    shift = table[:, feature_width:]
    tokens_f = tokens.reshape(row_count, feature_width).astype(jnp.float32)
    pre, pullback = jax.vjp(lambda value: normalize_modulate(value, shift, scale), tokens_f)
    normed = pre.astype(jnp.bfloat16)
    codes = gate_codes.reshape(row_count, top_count).astype(jnp.float32)
    route_weight = codes / jnp.sum(codes, axis=-1, keepdims=True)
    flat_routes = jnp.transpose(routes[0], (1, 0, 2)).reshape(row_count * top_count)
    expert_hot = (
        flat_routes[:, None] == jnp.arange(expert_count, dtype=jnp.int32)[None, :]
    ).astype(jnp.int32)
    earlier = jnp.cumsum(expert_hot, axis=0) - expert_hot
    position = jnp.sum(earlier * expert_hot, axis=1)
    slot_ids = flat_routes * capacity + position
    slot_hot = (slot_ids[:, None] == jnp.arange(slot_count, dtype=jnp.int32)[None, :]).astype(
        jnp.float32
    )
    slot_hot = slot_hot.reshape(row_count, top_count, slot_count)
    member = jnp.sum(slot_hot, axis=1)
    weighted = jnp.sum(slot_hot * route_weight[:, :, None], axis=1)
    contract_tokens = (((0,), (0,)), ((), ()))
    send_rows = lax.dot_general(
        member.astype(jnp.bfloat16), normed, contract_tokens, preferred_element_type=jnp.float32
    ).astype(jnp.bfloat16)
    grads_f = cotangent.reshape(row_count, feature_width).astype(jnp.float32)
    send_grads = lax.dot_general(
        weighted, grads_f, contract_tokens, precision=lax.Precision.HIGHEST
    ).astype(jnp.bfloat16)
    send_rows = send_rows.reshape(n_exp, local_experts * capacity, feature_width)
    send_grads = send_grads.reshape(n_exp, local_experts * capacity, feature_width)
    arrived_rows, arrived_grads = in_one_piece((send_rows, send_grads), "exp", 0, 0, 1)

    def by_expert(arrived):
        shaped = arrived.reshape(n_exp, local_experts, capacity, feature_width)
        return jnp.transpose(shaped, (1, 0, 2, 3)).reshape(
            local_experts, n_exp * capacity, feature_width
        )

    rows_all = by_expert(arrived_rows)
    grads_all = by_expert(arrived_grads)
    weight_stack = jnp.stack([gate_weight, up_weight, jnp.swapaxes(down_weight, 1, 2)], axis=1)
    piece = lax.all_gather(weight_stack, "seq", axis=3, tiled=True)
    count = piece.shape[3] // block_width
    shaped = piece.reshape(local_experts, 3, feature_width, count, block_width)
    gate_part = shaped[0, 0]
    up_part = shaped[0, 1]
    down_part = shaped[0, 2]
    rows_in = rows_all[0]
    grads_in = grads_all[0]
    gate_pre = jnp.einsum("rd,dkf->krf", rows_in, gate_part, preferred_element_type=jnp.float32)
    up_pre = jnp.einsum("rd,dkf->krf", rows_in, up_part, preferred_element_type=jnp.float32)
    grad_hidden = jnp.einsum("rd,dkf->krf", grads_in, down_part, preferred_element_type=jnp.float32)
    sigma = jax.nn.sigmoid(gate_pre)
    silu_gate = gate_pre * sigma
    grad_gate_pre = (grad_hidden * up_pre * sigma * (1.0 + gate_pre * (1.0 - sigma))).astype(
        jnp.bfloat16
    )
    grad_up_pre = (grad_hidden * silu_gate).astype(jnp.bfloat16)
    back_term = jnp.einsum(
        "krf,dkf->krd", grad_gate_pre, gate_part, preferred_element_type=jnp.float32
    )
    back_term = back_term + jnp.einsum(
        "krf,dkf->krd", grad_up_pre, up_part, preferred_element_type=jnp.float32
    )
    back_term = back_term.astype(jnp.bfloat16).astype(jnp.float32)
    results = [jnp.sum(back_term, axis=0)]
    folded = jnp.stack(results)
    folded = folded.reshape(local_experts, n_exp, capacity, feature_width)
    slot_source = jnp.transpose(folded, (1, 0, 2, 3)).reshape(
        n_exp, local_experts * capacity, feature_width
    )
    slot_source = slot_source.astype(jnp.bfloat16)
    slot_backs = lax.all_to_all(slot_source, "exp", split_axis=0, concat_axis=0, tiled=True)
    slot_backs = slot_backs.reshape(slot_count, feature_width).astype(jnp.float32)
    grad_normed = jnp.dot(member, slot_backs, precision=lax.Precision.HIGHEST)
    grad_tokens = pullback(grad_normed)[0]
    return grad_tokens.astype(jnp.bfloat16).reshape(img_local, patch_local, feature_width)


def solution(mesh):
    in_specs = (
        P("exp", "seq", None),
        P("exp"),
        P(),
        P("exp", "seq", None, None),
        P("exp", "seq", None),
        P("exp", None, "seq"),
        P("exp", None, "seq"),
        P("exp", "seq", None),
        P("exp", "seq", None),
    )
    out_specs = P("exp", "seq", None)
    return jax.shard_map(
        per_device, mesh=mesh, in_specs=in_specs, out_specs=out_specs, check_vma=False
    )
```

profile of v0, /device:TPU:1, one launch (start us, length us, event | category | flops | bytes accessed | tf_op | source)
XLA Modules:
  0.0 319.6 jit_solution(1848872654035132093)
XLA Ops:
  6.5 0.0 copy-start
  6.5 0.0 copy-start.2
  6.5 0.0 copy-start.5
  6.5 0.0 copy-start.6
  6.5 0.0 all-gather.2.cloned.1.call-start
  6.6 3.1 pad_maximum_fusion
  9.7 0.0 all-gather.2.cloned.1.call-update
  9.7 0.8 copy.19
  10.5 0.1 eq.56
  10.6 0.1 eq.52
  10.8 0.7 convert_element_type.73
  11.5 0.7 convert_reduce_fusion.1
  12.2 0.1 div.59
  12.2 1.1 fusion.22
  13.3 0.1 sqrt.19
  13.4 0.7 broadcast_multiply_fusion
  14.1 0.1 mul.83
  14.2 0.1 convert_element_type.74
  14.3 0.6 reduce-window.6
  14.9 0.2 slice_reduce_fusion
  15.1 0.1 fusion.28
  15.2 0.1 reduce_sum.73
  15.3 0.1 copy.22
  15.4 0.0 copy-done.5
  15.4 0.1 copy.25
  15.5 0.1 select_reduce_fusion
  15.6 0.0 copy-done
  15.6 0.0 copy-start.3
  15.6 0.7 convolution_convert_fusion
  16.2 0.2 reshape.138
  16.5 0.0 copy-done.6
  16.5 0.2 fusion.30
  16.7 0.1 broadcast_in_dim.6
  16.8 0.0 copy-done.2
  16.8 0.2 fusion.21
  17.0 0.0 copy-done.3
  17.0 1.2 convolution_convert_fusion.1
  18.1 1.3 reshape.136
  19.4 0.3 pad_maximum_fusion.1
  19.7 47.3 %all_to_all.10 = bf16[16,34,1152]{2,1,0:T(8,128)(2,1)S(1)} all-to-all(bf16[16,34,1152]{2,1,0:T(8,128)(2,1)S(1)} %pad_maximum_fusion.1), channel_id=1, replica_groups=mesh['seq'=16,'exp'=16] {'exp'}, dimensions={0} | all-to-all | bytes 2506752 | tf_op jit(solution)/shard_map/all_to_all | solution.py:15
  67.1 0.2 fusion.37
  67.3 1.1 reshape.142
  68.4 0.2 reshape.143
  68.6 138.1 %all-gather.2.cloned.1.call-done = bf16[1,3,1152,4608]{2,3,1,0:T(8,128)(2,1)} async-done(((bf16[1,3,1152,288]{2,3,1,0:T(8,128)(2,1)}), bf16[1,3,1152,4608]{2,3,1,0:T(8,128)(2,1)}) %all-gather.2.cloned.1.call-update) | async-done | bytes 31850512 | tf_op jit(solution)/shard_map/all_gather | solution.py:100
  206.7 14.3 %fusion = f32[16,288,272]{1,2,0:T(8,128)} fusion(bf16[272,1152,1]{1,0,2:T(8,128)(2,1)} %reshape.142, bf16[1,3,1152,16,288]{2,4,3,1,0:T(8,128)(2,1)} %bitcast.127), kind=kOutput, calls=%fused_computation.4 | convolution fusion | flops 2887778304 | bytes 16257024 | tf_op jit(solution)/shard_map/rd,dkf->krf/dot_general | solution.py:110
  221.0 14.3 %fusion.3 = f32[16,288,272]{1,2,0:T(8,128)} fusion(bf16[272,1152,1]{1,0,2:T(8,128)(2,1)S(1)} %reshape.143, bf16[1,3,1152,16,288]{2,4,3,1,0:T(8,128)(2,1)} %bitcast.128), kind=kOutput, calls=%fused_computation.7 | convolution fusion | flops 2887778304 | bytes 16257024 | tf_op jit(solution)/shard_map/rd,dkf->krf/dot_general | solution.py:108
  235.3 24.0 %fusion.2 = f32[16,272,1152]{2,1,0:T(8,128)} fusion(bf16[1,3,1152,16,288]{2,4,3,1,0:T(8,128)(2,1)} %bitcast.129, f32[16,288,272]{1,2,0:T(8,128)} %fusion.3, f32[16,288,272]{1,2,0:T(8,128)} %fusion, bf16[272,1152,1]{1,0,2:T(8,128)(2,1)S(1)} %reshape.143), kind=kOutput, calls=%fused_computation.6 | convolution fusion | flops 5788090368 | bytes 55283712 | tf_op jit(solution)/shard_map/krf,dkf->krd/dot_general | solution.py:117
  259.3 0.0 copy-start.4
  259.3 0.0 copy-start.1
  259.3 17.7 %fusion.17 = bf16[272,1152]{1,0:T(8,128)(2,1)S(1)} fusion(f32[16,272,1152]{2,1,0:T(8,128)} %fusion.2, bf16[1,3,1152,16,288]{2,4,3,1,0:T(8,128)(2,1)} %bitcast.130, f32[16,288,272]{1,2,0:T(8,128)} %fusion.3, f32[16,288,272]{1,2,0:T(8,128)} %fusion), kind=kOutput, calls=%fused_computation.27 | convolution fusion | flops 2910025728 | bytes 44666880 | tf_op jit(solution)/shard_map/krf,dkf->krd/dot_general | solution.py:120
  277.0 1.1 convert_element_type.79
  278.1 7.9 %all-to-all-start.1 = ((bf16[16,17,1152]{2,1,0:T(8,128)(2,1)}), bf16[16,17,1152]{2,1,0:T(8,128)(2,1)S(1)}, u32[]{:S(2)}, u32[]{:S(2)}) async-start(bf16[16,17,1152]{2,1,0:T(8,128)(2,1)} %convert_element_type.79), calls=%async_computation.1 | async-start | bytes 1769472 | tf_op jit(solution)/shard_map/all_to_all | solution.py:131
  286.0 0.1 div.67
  286.1 24.6 %all-to-all-done.1 = bf16[16,17,1152]{2,1,0:T(8,128)(2,1)S(1)} async-done(((bf16[16,17,1152]{2,1,0:T(8,128)(2,1)}), bf16[16,17,1152]{2,1,0:T(8,128)(2,1)S(1)}, u32[]{:S(2)}, u32[]{:S(2)}) %all-to-all-start.1) | async-done | bytes 626720 | tf_op jit(solution)/shard_map/all_to_all | solution.py:131
  310.7 0.2 reshape.139
  310.9 0.0 copy-done.4
  310.9 0.9 fusion.24
  311.8 0.9 fusion.20
  312.7 0.0 copy-done.1
  (10 shorter events, 0.1 us)
Async XLA Ops:
  6.5 9.0 %copy-start = (bf16[2,64,1152]{2,1,0:T(8,128)(2,1)S(1)}, bf16[2,64,1152]{2,1,0:T(8,128)(2,1)}, u32[]{:S(2)}) copy-start(bf16[2,64,1152]{2,1,0:T(8,128)(2,1)} %param.17) | copy-start | bytes 884740
  6.5 10.2 %copy-start.2 = (bf16[2,64,1152]{2,1,0:T(8,128)(2,1)S(1)}, bf16[2,64,1152]{2,1,0:T(8,128)(2,1)}, u32[]{:S(2)}) copy-start(bf16[2,64,1152]{2,1,0:T(8,128)(2,1)} %param.9) | copy-start | bytes 884740
  6.5 8.9 %copy-start.5 = (bf16[64,2,1152]{2,1,0:T(2,128)(2,1)S(1)}, bf16[64,2,1152]{2,1,0:T(2,128)(2,1)}, u32[]{:S(2)}) copy-start(bf16[64,2,1152]{2,1,0:T(2,128)(2,1)} %param.11) | copy-start | bytes 884740
  6.5 9.9 %copy-start.6 = (s32[2]{0:T(128)S(1)}, s32[2]{0:T(128)}, u32[]{:S(2)}) copy-start(s32[2]{0:T(128)} %param.10) | copy-start | bytes 28
  6.5 200.2 %all-gather.2.cloned.1.call-start = ((), (), s32[]{:S(2)}) async-start(), calls=%async_computation.2 | async-start | bytes 33841152 | tf_op jit(solution)/shard_map/all_gather | solution.py:100
  15.6 1.4 copy-start.3
  259.3 51.6 %copy-start.4 = (f32[128,272]{0,1:T(8,128)S(1)}, f32[128,272]{0,1:T(8,128)}, u32[]{:S(2)}) copy-start(f32[128,272]{0,1:T(8,128)} %copy-done.3) | copy-start | bytes 417796
  259.3 53.4 %copy-start.1 = (bf16[2,64,1152]{2,1,0:T(8,128)(2,1)S(1)}, bf16[2,64,1152]{2,1,0:T(8,128)(2,1)}, u32[]{:S(2)}) copy-start(bf16[2,64,1152]{2,1,0:T(8,128)(2,1)} %param.17) | copy-start | bytes 884740
  278.1 32.6 %all-to-all-start.1 = ((bf16[16,17,1152]{2,1,0:T(8,128)(2,1)}), bf16[16,17,1152]{2,1,0:T(8,128)(2,1)S(1)}, u32[]{:S(2)}, u32[]{:S(2)}) async-start(bf16[16,17,1152]{2,1,0:T(8,128)(2,1)} %convert_element_type.79), calls=%async_computation.1 | async-start | bytes 1769472 | tf_op jit(solution)/shard_map/all_to_all | solution.py:131
Sparse Core Ops, SparseCore 0:
  9.8 196.8 all-gather.1
where the time goes:
time: 320 us
  waiting for transfers between devices  163 us (51%)
  matrix products  73.1 us (23%)
  blocking collectives  47.3 us (15%)
  between operations  13.6 us (4%)
  other arithmetic  8.44 us (3%)
  starting transfers between devices  7.89 us (2%)
  local copies, waits for them, and re-layouts  6.47 us (2%)
    all_gather x1, waiting for transfers between devices, per_device(): piece = lax.all_gather(weight_stack, 'seq', axis=3, tiled=True)  138 us
    all_to_all x1, blocking collectives, in_one_piece(): lax.all_to_all(both, axis, split_axis=split_dim, concat_axis=concat_dim,...  47.3 us
    all_to_all x1, waiting for transfers between devices, per_device(): lax.all_to_all(slot_source, 'exp', split_axis=0, concat_axis=0, tiled=True)  24.6 us
    dot_general x1, matrix products, per_device(): jnp.einsum('krf,dkf->krd', grad_gate_pre, gate_part, preferred_element_ty...  24 us
    dot_general x1, matrix products, per_device(): jnp.einsum('krf,dkf->krd', grad_up_pre, up_part, preferred_element_type=j...  17.7 us
    dot_general x1, matrix products, per_device(): jnp.einsum('rd,dkf->krf', grads_in, down_part, preferred_element_type=jnp...  14.3 us
    dot_general x1, matrix products, per_device(): jnp.einsum('rd,dkf->krf', rows_in, gate_part, preferred_element_type=jnp....  14.3 us
    all_to_all x1, starting transfers between devices, per_device(): lax.all_to_all(slot_source, 'exp', split_axis=0, concat_axis=0, tiled=True)  7.86 us
  transfers between devices with their start and end apart: 2, of which 2 were waited for; matrix products, arithmetic and copies ran while one was open for 4% of the time, Pallas kernels for 0%

commit v1 on v0

--- a/solution.py
+++ b/solution.py
@@ -97,7 +97,15 @@
     rows_all = by_expert(arrived_rows)
     grads_all = by_expert(arrived_grads)
     weight_stack = jnp.stack([gate_weight, up_weight, jnp.swapaxes(down_weight, 1, 2)], axis=1)
-    piece = lax.all_gather(weight_stack, "seq", axis=3, tiled=True)
+    piece = jnp.concatenate(
+        lax.all_to_all(
+            jnp.stack([weight_stack for _ in range(lax.axis_size("seq"))]),
+            axis_name="seq",
+            split_axis=0,
+            concat_axis=0,
+        ),
+        3,
+    )
     count = piece.shape[3] // block_width
     shaped = piece.reshape(local_experts, 3, feature_width, count, block_width)
     gate_part = shaped[0, 0]

time: 320 us -> 810 us (2.53)
  waiting for transfers between devices: 163 us -> 661 us
  blocking collectives: 47.3 us -> 0 us
  local copies, waits for them, and re-layouts: 6.47 us -> 41.3 us
  between operations: 13.6 us -> 0.2 us
  starting transfers between devices: 7.89 us -> 20.3 us
    all_to_all x0 -> x2, waiting for transfers between devices: none -> 637 us  [the longest x1 602 us: per_device(): lax.all_to_all(jnp.stack([weight_stack for _ in range(lax.axis_size('seq'...]
    all_gather x1 -> x0, waiting for transfers between devices: 138 us -> none  [per_device(): piece = lax.all_gather(weight_stack, 'seq', axis=3, tiled=True)]
    all_to_all x1 -> x0, blocking collectives: 47.3 us -> none  [in_one_piece(): lax.all_to_all(both, axis, split_axis=split_dim, concat_axis=concat_dim,...]
    all_to_all x0 -> x1, local copies, waits for them, and re-layouts: none -> 22 us  [per_device(): lax.all_to_all(jnp.stack([weight_stack for _ in range(lax.axis_size('seq'...]
    all_to_all x0 -> x2, starting transfers between devices: none -> 16.8 us  [the longest x1 9.97 us: in_one_piece(): lax.all_to_all(both, axis, split_axis=split_dim, concat_axis=concat_dim,...]
    another operation x1 -> x2, local copies, waits for them, and re-layouts: 0.01 us -> 10.4 us  [the longest x1 10.4 us: per_device(): jnp.stack([weight_stack for _ in range(lax.axis_size('seq'))])]
  transfers between devices with their start and end apart: 2 -> 3, of which waited for: 2 -> 3; matrix products, arithmetic and copies ran while one was open for 4% -> 1% of each run, Pallas kernels for 0% -> 0%
where the time goes in v1:
time: 810 us; the launch traced here: 806 us
  waiting for transfers between devices  661 us (82%)
  matrix products  73.9 us (9%)
  local copies, waits for them, and re-layouts  41.3 us (5%)
  starting transfers between devices  20.3 us (3%)
  other arithmetic  9.28 us (1%)
    all_to_all x1, waiting for transfers between devices, per_device(): lax.all_to_all(jnp.stack([weight_stack for _ in range(lax.axis_size('seq'...  602 us
    all_to_all x1, waiting for transfers between devices, in_one_piece(): lax.all_to_all(both, axis, split_axis=split_dim, concat_axis=concat_dim,...  34.9 us
    all_to_all x1, waiting for transfers between devices, per_device(): lax.all_to_all(slot_source, 'exp', split_axis=0, concat_axis=0, tiled=True)  24.5 us
    dot_general x1, matrix products, per_device(): jnp.einsum('krf,dkf->krd', grad_gate_pre, gate_part, preferred_element_ty...  24 us
    all_to_all x1, local copies, waits for them, and re-layouts, per_device(): lax.all_to_all(jnp.stack([weight_stack for _ in range(lax.axis_size('seq'...  22 us
    dot_general x1, matrix products, per_device(): jnp.einsum('krf,dkf->krd', grad_up_pre, up_part, preferred_element_type=j...  17.9 us
  transfers between devices with their start and end apart: 3, of which 3 were waited for; matrix products, arithmetic and copies ran while one was open for 1% of the time, Pallas kernels for 0%

profile of v1, /device:TPU:1, one launch (start us, length us, event | category | flops | bytes accessed | tf_op | source)
XLA Modules:
  0.0 806.1 jit_solution(5502850105059017408)
XLA Ops:
  0.0 0.0 copy-start
  0.0 0.7 convert_reduce_fusion.1
  0.7 0.7 convert_element_type.73
  1.4 0.7 broadcast_multiply_fusion
  2.1 0.8 copy.28
  2.9 0.1 eq.56
  3.0 0.1 eq.52
  3.2 0.1 div.59
  3.3 1.1 fusion.22
  4.4 0.1 sqrt.19
  4.5 0.1 mul.83
  4.6 0.1 convert_element_type.74
  4.6 0.6 reduce-window.6
  5.2 0.2 slice_reduce_fusion
  5.5 0.1 fusion.28
  5.5 0.1 reduce_sum.73
  5.7 0.1 copy.31
  5.8 1.0 copy.35
  6.8 0.1 select_reduce_fusion
  6.9 0.0 copy-done
  6.9 0.0 copy-start.3
  6.9 0.6 convolution_convert_fusion
  7.5 0.2 reshape.141
  7.8 0.9 fusion.30
  8.6 0.1 broadcast_in_dim.6
  8.7 1.2 fusion.21
  9.9 0.0 copy-done.3
  9.9 1.1 convolution_convert_fusion.1
  11.0 1.3 reshape.139
  12.3 1.4 pad_maximum_fusion
  13.8 10.0 %all-to-all-start.1 = ((bf16[16,34,1152]{2,1,0:T(8,128)(2,1)}), bf16[16,34,1152]{2,1,0:T(8,128)(2,1)}, u32[]{:S(2)}, u32[]{:S(2)}) async-start(bf16[16,34,1152]{2,1,0:T(8,128)(2,1)} %pad_maximum_fusion), calls=%async_computation.1 | async-start | bytes 2949120 | tf_op jit(solution)/shard_map/all_to_all | solution.py:15
  23.7 1.8 maximum_bitcast_fusion
  25.5 34.9 %all-to-all-done.1 = bf16[16,34,1152]{2,1,0:T(8,128)(2,1)} async-done(((bf16[16,34,1152]{2,1,0:T(8,128)(2,1)}), bf16[16,34,1152]{2,1,0:T(8,128)(2,1)}, u32[]{:S(2)}, u32[]{:S(2)}) %all-to-all-start.1) | async-done | bytes 1253408 | tf_op jit(solution)/shard_map/all_to_all | solution.py:15
  60.4 10.4 %stack.17 = bf16[16,1,3,1152,288]{3,4,2,1,0:T(8,128)(2,1)} broadcast(bf16[3,1152,288]{1,2,0:T(8,128)(2,1)S(1)} %maximum_bitcast_fusion), dimensions={2,3,4} | broadcast | bytes 33841152 | tf_op jit(solution)/shard_map/stack | solution.py:102
  70.8 6.8 all-to-all-start
  77.6 1.7 fusion.37
  79.3 1.1 reshape.145
  80.4 0.2 reshape.146
  80.6 0.0 copy-start.5
  80.6 601.8 %all-to-all-done = bf16[16,1,3,1152,288]{3,4,2,1,0:T(8,128)(2,1)} async-done(((bf16[16,1,3,1152,288]{3,4,2,1,0:T(8,128)(2,1)}), bf16[16,1,3,1152,288]{3,4,2,1,0:T(8,128)(2,1)}, u32[]{:S(2)}, u32[]{:S(2)}) %all-to-all-start) | async-done | bytes 31850528 | tf_op jit(solution)/shard_map/all_to_all | solution.py:101
  682.4 22.0 %copy.38 = bf16[16,1,3,1152,288]{3,4,0,2,1:T(8,128)(2,1)} copy(bf16[16,1,3,1152,288]{3,4,2,1,0:T(8,128)(2,1)} %all-to-all-done) | data formatting | bytes 63700992 | tf_op jit(solution)/shard_map/all_to_all | solution.py:101
  704.4 0.0 copy-done.5
  704.4 14.3 %fusion = f32[16,288,272]{1,2,0:T(8,128)} fusion(bf16[272,1152,1]{1,0,2:T(8,128)(2,1)S(1)} %copy-done.5, bf16[1,3,1152,16,288]{2,4,3,1,0:T(8,128)(2,1)} %bitcast.123), kind=kOutput, calls=%fused_computation.5 | convolution fusion | flops 2887778304 | bytes 16257024 | tf_op jit(solution)/shard_map/rd,dkf->krf/dot_general | solution.py:118
  718.7 14.2 %fusion.3 = f32[16,288,272]{1,2,0:T(8,128)} fusion(bf16[272,1152,1]{1,0,2:T(8,128)(2,1)S(1)} %reshape.146, bf16[1,3,1152,16,288]{2,4,3,1,0:T(8,128)(2,1)} %bitcast.124), kind=kOutput, calls=%fused_computation.8 | convolution fusion | flops 2887778304 | bytes 16257024 | tf_op jit(solution)/shard_map/rd,dkf->krf/dot_general | solution.py:116
  732.9 24.0 %fusion.2 = f32[16,272,1152]{2,1,0:T(8,128)} fusion(bf16[1,3,1152,16,288]{2,4,3,1,0:T(8,128)(2,1)} %bitcast.125, f32[16,288,272]{1,2,0:T(8,128)} %fusion.3, f32[16,288,272]{1,2,0:T(8,128)} %fusion, bf16[272,1152,1]{1,0,2:T(8,128)(2,1)S(1)} %reshape.146), kind=kOutput, calls=%fused_computation.7 | convolution fusion | flops 5788090368 | bytes 55283712 | tf_op jit(solution)/shard_map/krf,dkf->krd/dot_general | solution.py:125
  756.9 0.0 copy-start.2
  756.9 0.0 copy-start.4
  756.9 0.0 copy-start.1
  756.9 17.9 %fusion.17 = bf16[272,1152]{1,0:T(8,128)(2,1)S(1)} fusion(f32[16,272,1152]{2,1,0:T(8,128)} %fusion.2, bf16[1,3,1152,16,288]{2,4,3,1,0:T(8,128)(2,1)} %bitcast.126, f32[16,288,272]{1,2,0:T(8,128)} %fusion.3, f32[16,288,272]{1,2,0:T(8,128)} %fusion), kind=kOutput, calls=%fused_computation.28 | convolution fusion | flops 2910025728 | bytes 44666880 | tf_op jit(solution)/shard_map/krf,dkf->krd/dot_general | solution.py:128
  774.8 1.1 convert_element_type.79
  775.9 3.5 all-to-all-start.2
  779.5 0.1 div.67
  779.5 24.5 %all-to-all-done.2 = bf16[16,17,1152]{2,1,0:T(8,128)(2,1)S(1)} async-done(((bf16[16,17,1152]{2,1,0:T(8,128)(2,1)}), bf16[16,17,1152]{2,1,0:T(8,128)(2,1)S(1)}, u32[]{:S(2)}, u32[]{:S(2)}) %all-to-all-start.2) | async-done | bytes 626720 | tf_op jit(solution)/shard_map/all_to_all | solution.py:139
  804.0 0.2 reshape.142
  804.2 0.0 copy-done.2
  804.2 0.0 copy-done.4
  804.3 0.9 fusion.24
  805.1 0.9 fusion.20
  806.1 0.0 copy-done.1
  (10 shorter events, 0.1 us)
Async XLA Ops:
  0.0 6.9 copy-start
  6.9 3.0 copy-start.3
  13.8 46.6 %all-to-all-start.1 = ((bf16[16,34,1152]{2,1,0:T(8,128)(2,1)}), bf16[16,34,1152]{2,1,0:T(8,128)(2,1)}, u32[]{:S(2)}, u32[]{:S(2)}) async-start(bf16[16,34,1152]{2,1,0:T(8,128)(2,1)} %pad_maximum_fusion), calls=%async_computation.1 | async-start | bytes 2949120 | tf_op jit(solution)/shard_map/all_to_all | solution.py:15
  70.8 611.6 %all-to-all-start = ((bf16[16,1,3,1152,288]{3,4,2,1,0:T(8,128)(2,1)}), bf16[16,1,3,1152,288]{3,4,2,1,0:T(8,128)(2,1)}, u32[]{:S(2)}, u32[]{:S(2)}) async-start(bf16[16,1,3,1152,288]{3,4,2,1,0:T(8,128)(2,1)} %stack.17), calls=%async_computation | async-start | bytes 63700992 | tf_op jit(solution)/shard_map/all_to_all | solution.py:101
  80.6 623.8 %copy-start.5 = (bf16[272,1152,1]{1,0,2:T(8,128)(2,1)S(1)}, bf16[272,1152,1]{1,0,2:T(8,128)(2,1)}, u32[]{:S(2)}) copy-start(bf16[272,1152,1]{1,0,2:T(8,128)(2,1)} %reshape.145) | copy-start | bytes 1880068
  756.9 47.4 %copy-start.2 = (bf16[2,64,1152]{2,1,0:T(8,128)(2,1)S(1)}, bf16[2,64,1152]{2,1,0:T(8,128)(2,1)}, u32[]{:S(2)}) copy-start(bf16[2,64,1152]{2,1,0:T(8,128)(2,1)} %param.9) | copy-start | bytes 884740
  756.9 47.4 %copy-start.4 = (f32[128,272]{0,1:T(8,128)S(1)}, f32[128,272]{0,1:T(8,128)}, u32[]{:S(2)}) copy-start(f32[128,272]{0,1:T(8,128)} %copy-done.3) | copy-start | bytes 417796
  756.9 49.2 %copy-start.1 = (bf16[2,64,1152]{2,1,0:T(8,128)(2,1)S(1)}, bf16[2,64,1152]{2,1,0:T(8,128)(2,1)}, u32[]{:S(2)}) copy-start(bf16[2,64,1152]{2,1,0:T(8,128)(2,1)} %param.17) | copy-start | bytes 884740
  775.9 28.1 %all-to-all-start.2 = ((bf16[16,17,1152]{2,1,0:T(8,128)(2,1)}), bf16[16,17,1152]{2,1,0:T(8,128)(2,1)S(1)}, u32[]{:S(2)}, u32[]{:S(2)}) async-start(bf16[16,17,1152]{2,1,0:T(8,128)(2,1)} %convert_element_type.79), calls=%async_computation.2 | async-start | bytes 1769472 | tf_op jit(solution)/shard_map/all_to_all | solution.py:139
